TPU v7x, 512 devices: a whole 4x8x8 slice. The times are simulated.
512 devices in a mesh: imp: 32 (over z, x), adv: 16 (over y, core).
Axes of the slice: x: 4, y: 8, z: 8, core: 2. Of those that a mesh axis runs over, the one named last changes fastest.
Arguments:
- impression_vectors: bfloat16 [64, 65536], P(None, 'imp'), may hold values from -6 to 6
- advertiser_vectors: bfloat16 [64, 65536], P(None, ('imp', 'adv')), may hold values from -0.75 to 0.75
- spend_limits: float32 [65536], P(('imp', 'adv')), may hold values from 1024 to 8192
- capacity: float32 [65536], P('imp'), may hold values from 1024 to 8192
- blocks: int32 [512, 16, 8], P('imp', 'adv'), may hold values from 0 to 511, as said below
- counts: int32 [512, 16], P('imp', 'adv'), may hold values from 1 to 8, as said below
Outputs:
- prices: float32 [65536], P(('imp', 'adv'))
- impression_duals: float32 [65536], P('imp')
- impression_grad: bfloat16 [64, 65536], P(None, ('imp', 'adv'))
- advertiser_grad: bfloat16 [64, 65536], P(None, ('imp', 'adv'))
Inputs may be any that keep to these rules, and one draw needn't show every extreme that they name: Block numbers. Entry [g, a, k] names a block b with (b) % (the size of adv) == a. The 8 entries of one list are distinct; entries at slots k >= counts[g, a] are padding and name valid blocks too. `counts`: every group has one index of adv whose count is 8.
All inputs are finite; a program needn't handle non-finite values.
Results may differ from a plain program's by a relative error of at most 0.012.
Values may be sent and summed in bfloat16 or wider, within the bound.
No kernel may reach another device: no remote copies, remote signals or barrier semaphores. Data moves between devices by JAX's collectives and lax.ppermute only.
A program may use at most 64 MiB of HBM per device.

v0:
```python
import jax
import jax.numpy as jnp
from jax import lax
from jax.sharding import PartitionSpec as P

GROUP = 128
BLOCK = 128
ITERS = 3
BLK_DEV = 1


def local(impression_vectors, advertiser_vectors, spend_limits, capacity, blocks, counts):
    features = impression_vectors.shape[0]
    groups_here = blocks.shape[0]
    slot_count = blocks.shape[2]
    adv_devices = lax.axis_size("adv")
    block_ids = blocks.reshape(groups_here, slot_count)
    local_ids = block_ids // BLK_DEV // adv_devices * BLK_DEV + block_ids % BLK_DEV
    live_slots = (jnp.arange(slot_count)[None, :] < counts).astype(jnp.float32)
    viewers = impression_vectors.reshape(features, groups_here, GROUP)
    extent = slot_count * BLOCK
    own_count = spend_limits.shape[0]
    fetched = lax.all_gather(advertiser_vectors, "imp", axis=1, tiled=True)
    catalog = fetched.reshape(features, fetched.shape[1] // BLOCK, BLOCK)
    local_blocks = catalog.shape[1]

    def allocate(source, prices, duals, group_no):
        chosen = lax.dynamic_index_in_dim(local_ids, group_no, 0, keepdims=False)
        columns = jnp.take(source, chosen, axis=1).reshape(features, extent)
        viewer = lax.dynamic_index_in_dim(viewers, group_no, 1, keepdims=False)
        scores = lax.dot_general(
            viewer, columns, (((0,), (0,)), ((), ())), preferred_element_type=jnp.float32
        )
        charged = jnp.take(prices, chosen, axis=0).reshape(extent)
        shadow = lax.dynamic_slice_in_dim(duals, group_no * GROUP, GROUP)
        eligible = jnp.repeat(
            lax.dynamic_index_in_dim(live_slots, group_no, 0, keepdims=False), BLOCK
        )
        shares = jnp.clip(scores - charged[None, :] - shadow[:, None], 0.0, 1.0) * eligible[None, :]
        return (shares, chosen, columns, viewer)

    duals = jnp.zeros((groups_here * GROUP,), jnp.float32)
    range_prices = jnp.zeros((local_blocks, BLOCK), jnp.float32)
    own_prices = jnp.zeros((own_count,), jnp.float32)
    for iteration in range(ITERS):
        totals_prices = range_prices

        def advance(group_no, pair):
            outlay, demand = pair
            shares, chosen, _, _ = allocate(catalog, totals_prices, duals, group_no)
            outlay = outlay.at[chosen].add(jnp.sum(shares, axis=0).reshape(slot_count, BLOCK))
            demand = lax.dynamic_update_slice_in_dim(
                demand, jnp.sum(shares, axis=1), group_no * GROUP, 0
            )
            return (outlay, demand)

        totals_start = (
            jnp.zeros((local_blocks, BLOCK), jnp.float32),
            jnp.zeros((groups_here * GROUP,), jnp.float32),
        )
        outlay, demand = lax.fori_loop(0, groups_here, advance, totals_start)
        own_outlay = lax.psum_scatter(outlay.reshape(-1), "imp", scatter_dimension=0, tiled=True)
        dual_demand = demand
        dual_demand = lax.psum(dual_demand, "adv")
        duals = jnp.maximum(duals + dual_demand / capacity - 1.0, 0.0)
        own_prices = jnp.maximum(own_prices + own_outlay / spend_limits - 1.0, 0.0)
        range_prices = lax.all_gather(own_prices, "imp", axis=0, tiled=True).reshape(
            local_blocks, BLOCK
        )

    def grad_step(group_no, pair):
        imp_part, adv_part = pair
        shares, chosen, columns, viewer = allocate(catalog, range_prices, duals, group_no)
        weights = shares.astype(jnp.bfloat16)
        imp_cols = lax.dot_general(
            columns, weights, (((1,), (1,)), ((), ())), preferred_element_type=jnp.float32
        )
        imp_part = lax.dynamic_update_slice_in_dim(imp_part, imp_cols, group_no * GROUP, 1)
        adv_terms = jnp.dot(viewer, weights, preferred_element_type=jnp.float32).reshape(
            features, slot_count, BLOCK
        )
        adv_part = adv_part.at[:, chosen].add(adv_terms)
        return (imp_part, adv_part)

    start = (
        jnp.zeros((features, groups_here * GROUP), jnp.float32),
        jnp.zeros((features, local_blocks, BLOCK), jnp.float32),
    )
    imp_part, adv_part = lax.fori_loop(0, groups_here, grad_step, start)
    impression_grad = lax.psum_scatter(imp_part, "adv", scatter_dimension=1, tiled=True).astype(
        jnp.bfloat16
    )
    adv_rounded = (adv_part.reshape(features, -1) / GROUP).astype(jnp.bfloat16)
    advertiser_grad = (
        lax.psum_scatter(adv_rounded, "imp", scatter_dimension=1, tiled=True)
        .astype(jnp.float32)
        .astype(jnp.bfloat16)
    )
    return (own_prices, duals, impression_grad, advertiser_grad)


def solution(mesh):
    return jax.shard_map(
        local,
        mesh=mesh,
        in_specs=(
            P(None, "imp"),
            P(None, ("imp", "adv")),
            P(("imp", "adv")),
            P("imp"),
            P("imp", "adv", None),
            P("imp", "adv"),
        ),
        out_specs=(P(("imp", "adv")), P("imp"), P(None, ("imp", "adv")), P(None, ("imp", "adv"))),
        check_vma=False,
    )
```

profile of v0, /device:TPU:25, one launch (start us, length us, event | category | flops | bytes accessed | tf_op | source)
XLA Modules:
  0.0 1180.3 jit_solution(11911110707107156288)
XLA Ops:
  7.2 0.7 copy-done.12
  8.0 0.7 copy-done.14
  8.8 0.6 copy-done.7
  9.5 44.2 %all_gather.12 = bf16[64,4096]{1,0:T(8,128)(2,1)S(1)} all-gather(bf16[64,128]{1,0:T(8,128)(2,1)S(1)} %copy-done.7), channel_id=1, replica_groups=mesh['imp'=32,'adv'=16] {'imp'}, dimensions={1}, use_global_device_ids=true | all-gather | bytes 540672 | tf_op jit(solution)/shard_map/all_gather | solution.py:23
  53.8 41.5 %while.60 = (s32[]{:T(128)}, f32[32,128]{1,0:T(8,128)S(1)}, f32[2048]{0:T(1024)S(1)}, s32[16,8]{1,0:T(8,128)S(1)}, bf16[64,16,128]{2,0,1:T(8,128)(2,1)S(1)}, /*i...) while((s32[]{:T(128)}, f32[32,128]{1,0:T(8,128)S(1)}, ...), condition=%wide.region_4.7_spmd, body=%wide.region_0.6_spmd.sunk | while | flops 17500104 | bytes 485907 | solution.py:61
  79.3 0.6 scatter_custom_fusion.15
  81.8 0.6 scatter_custom_fusion.15
  92.2 0.6 scatter_custom_fusion.15
  95.4 35.8 %psum.21 = f32[2048]{0:T(1024)S(1)} all-reduce(f32[2048]{0:T(1024)S(1)} %get-tuple-element.597), channel_id=1, replica_groups=mesh['imp'=32,'adv'=16] {'adv'}, use_global_device_ids=true, to_apply=%region_6.9 | all-reduce | flops 2048 | bytes 16384 | tf_op jit(solution)/shard_map/psum | solution.py:64
  131.2 112.5 %all-reduce = f32[4096]{0:T(1024)S(1)} all-reduce(f32[4096]{0:T(1024)S(1)} %bitcast.255), channel_id=2, replica_groups=mesh['imp'=32,'adv'=16] {'imp'}, use_global_device_ids=true, to_apply=%region_5.8.clone | all-reduce | flops 4096 | bytes 32768
  243.8 1.3 dynamic-slice
  245.8 28.0 %all-gather = f32[32,1,128]{2,1,0:T(1,128)S(1)} all-gather(f32[1,1,128]{2,1,0:T(1,128)S(1)} %bitcast.260), channel_id=1, replica_groups=mesh['imp'=32,'adv'=16] {'imp'}, dimensions={0}, use_global_device_ids=true | all-gather | bytes 16896 | tf_op jit(solution)/shard_map/all_gather | solution.py:67
  273.8 42.5 %while.61 = (s32[]{:T(128)}, f32[32,128]{1,0:T(8,128)S(1)}, f32[2048]{0:T(1024)S(1)}, s32[16,8]{1,0:T(8,128)S(1)}, bf16[64,16,128]{2,0,1:T(8,128)(2,1)S(1)}, /*i...) while((s32[]{:T(128)}, f32[32,128]{1,0:T(8,128)S(1)}, ...), condition=%wide.region_11.14_spmd, body=%wide.region_7.13_spmd.sunk | while | flops 17631180 | bytes 471067 | solution.py:61
  278.5 0.6 scatter_custom_fusion.17
  302.5 0.6 scatter_custom_fusion.17
  307.8 0.6 scatter_custom_fusion.17
  313.0 0.6 scatter_custom_fusion.17
  316.3 58.5 %psum.22 = f32[2048]{0:T(1024)S(1)} all-reduce(f32[2048]{0:T(1024)S(1)} %get-tuple-element.599), channel_id=1, replica_groups=mesh['imp'=32,'adv'=16] {'adv'}, use_global_device_ids=true, to_apply=%region_13.16 | all-reduce | flops 2048 | bytes 16384 | tf_op jit(solution)/shard_map/psum | solution.py:64
  374.8 112.3 %all-reduce.1 = f32[4096]{0:T(1024)S(1)} all-reduce(f32[4096]{0:T(1024)S(1)} %bitcast.256), channel_id=3, replica_groups=mesh['imp'=32,'adv'=16] {'imp'}, use_global_device_ids=true, to_apply=%region_12.15.clone | all-reduce | flops 4096 | bytes 32768
  487.2 27.5 %all-gather.1 = f32[32,1,128]{2,1,0:T(1,128)S(1)} all-gather(f32[1,1,128]{2,1,0:T(1,128)S(1)} %bitcast.259), channel_id=1, replica_groups=mesh['imp'=32,'adv'=16] {'imp'}, dimensions={0}, use_global_device_ids=true | all-gather | bytes 16896 | tf_op jit(solution)/shard_map/all_gather | solution.py:67
  514.7 42.4 %while.62 = (s32[]{:T(128)}, f32[32,128]{1,0:T(8,128)S(1)}, f32[2048]{0:T(1024)S(1)}, s32[16,8]{1,0:T(8,128)S(1)}, bf16[64,16,128]{2,0,1:T(8,128)(2,1)S(1)}, /*i...) while((s32[]{:T(128)}, f32[32,128]{1,0:T(8,128)S(1)}, ...), condition=%wide.region_18.21_spmd, body=%wide.region_14.20_spmd.sunk | while | flops 17631180 | bytes 471067 | solution.py:61
  557.1 59.3 %psum.23 = f32[2048]{0:T(1024)S(1)} all-reduce(f32[2048]{0:T(1024)S(1)} %get-tuple-element.601), channel_id=1, replica_groups=mesh['imp'=32,'adv'=16] {'adv'}, use_global_device_ids=true, to_apply=%region_20.23 | all-reduce | flops 2048 | bytes 16384 | tf_op jit(solution)/shard_map/psum | solution.py:64
  617.1 111.9 %all-reduce.2 = f32[4096]{0:T(1024)S(1)} all-reduce(f32[4096]{0:T(1024)S(1)} %bitcast.257), channel_id=4, replica_groups=mesh['imp'=32,'adv'=16] {'imp'}, use_global_device_ids=true, to_apply=%region_19.22.clone | all-reduce | flops 4096 | bytes 32768
  729.6 27.5 %all-gather.2 = f32[32,1,128]{2,1,0:T(1,128)S(1)} all-gather(f32[1,1,128]{2,1,0:T(1,128)S(1)} %bitcast.261), channel_id=1, replica_groups=mesh['imp'=32,'adv'=16] {'imp'}, dimensions={0}, use_global_device_ids=true | all-gather | bytes 16896 | tf_op jit(solution)/shard_map/all_gather | solution.py:67
  757.2 95.1 %while.63 = (s32[]{:T(128)}, f32[64,2048]{1,0:T(8,128)S(1)}, f32[64,32,128]{2,0,1:T(8,128)S(1)}, s32[16,8]{1,0:T(8,128)S(1)}, bf16[64,32,128]{2,0,1:T(8,128)(2,1...) while((s32[]{:T(128)}, f32[64,2048]{1,0:T(8,128)S(1)}, ...), condition=%wide.region_23.26_spmd, body=%wide.region_21.25_spmd.sunk | while | flops 51185740 | bytes 2993603 | solution.py:89
  757.8 0.8 dynamic_slice.201
  762.2 0.9 scatter_fusion
  763.7 0.8 dynamic_slice.201
  768.2 0.9 scatter_fusion
  769.7 0.8 dynamic_slice.201
  774.1 0.9 scatter_fusion
  775.6 0.8 dynamic_slice.201
  780.0 0.9 scatter_fusion
  781.6 0.8 dynamic_slice.201
  786.0 0.9 scatter_fusion
  787.5 0.8 dynamic_slice.201
  791.9 0.9 scatter_fusion
  793.5 0.8 dynamic_slice.201
  797.9 0.9 scatter_fusion
  799.4 0.8 dynamic_slice.201
  803.8 0.9 scatter_fusion
  805.4 0.8 dynamic_slice.201
  809.8 0.9 scatter_fusion
  811.3 0.8 dynamic_slice.201
  815.7 0.9 scatter_fusion
  817.3 0.8 dynamic_slice.201
  821.7 0.9 scatter_fusion
  823.2 0.8 dynamic_slice.201
  827.6 0.9 scatter_fusion
  829.1 0.8 dynamic_slice.201
  833.6 0.9 scatter_fusion
  835.1 0.8 dynamic_slice.201
  839.5 0.9 scatter_fusion
  841.0 0.8 dynamic_slice.201
  845.4 0.9 scatter_fusion
  847.0 0.8 dynamic_slice.201
  851.4 0.9 scatter_fusion
  852.4 0.7 copy-done.1
  853.1 1.3 copy.68
  854.6 0.7 reduce-scatter.5.cloned.1.call-update
  855.3 250.8 %reduce-scatter.7.cloned.1.call-done = bf16[128,64]{1,0:T(8,128)(2,1)} async-done(((bf16[4096,64]{1,0:T(8,128)(2,1)}), bf16[128,64]{1,0:T(8,128)(2,1)}) %reduce-scatter.7.cloned.1.call-update) | async-done | bytes 16400
  1106.1 1.4 copy.67
  1107.5 64.6 %reduce-scatter.5.cloned.1.call-done = f32[64,128]{1,0:T(8,128)} async-done(((f32[64,2048]{1,0:T(8,128)}), f32[64,128]{1,0:T(8,128)}) %reduce-scatter.5.cloned.1.call-update) | async-done | bytes 32784 | tf_op jit(solution)/shard_map/reduce_scatter | solution.py:90
  1172.1 1.4 convert_element_type.23
  (956 shorter events, 187.8 us)
Async XLA Ops:
  7.2 1.6 copy-start
  7.2 1098.9 %reduce-scatter.7.cloned.1.call-start = ((), (), s32[]{:S(2)}) async-start(), calls=%async_computation.3 | async-start | bytes 1081344
  245.8 28.0 %copy-start.2 = (f32[2048]{0:T(1024)S(1)}, f32[2048]{0:T(1024)}, u32[]{:S(2)}) copy-start(f32[2048]{0:T(1024)} %param.21) | copy-start | bytes 24580
  757.2 2.0 copy-start.5
  759.2 1.2 copy-start.3
  762.2 0.9 copy-start.6
  762.2 0.9 copy-start.10
  763.1 2.0 copy-start.5
  765.1 1.2 copy-start.3
  768.2 0.9 copy-start.6
  768.2 0.9 copy-start.10
  769.1 2.0 copy-start.5
  771.1 1.2 copy-start.3
  774.1 0.9 copy-start.6
  774.1 0.9 copy-start.10
  775.0 2.0 copy-start.5
  777.0 1.2 copy-start.3
  780.0 0.9 copy-start.6
  780.0 0.9 copy-start.10
  781.0 2.0 copy-start.5
  783.0 1.2 copy-start.3
  786.0 0.9 copy-start.6
  786.0 0.9 copy-start.10
  786.9 2.0 copy-start.5
  788.9 1.2 copy-start.3
  791.9 0.9 copy-start.6
  791.9 0.9 copy-start.10
  792.9 2.0 copy-start.5
  794.8 1.2 copy-start.3
  797.9 0.9 copy-start.6
  797.9 0.9 copy-start.10
  798.8 2.0 copy-start.5
  800.8 1.2 copy-start.3
  803.8 0.9 copy-start.6
  803.8 0.9 copy-start.10
  804.8 2.0 copy-start.5
  806.7 1.2 copy-start.3
  809.8 0.9 copy-start.6
  809.8 0.9 copy-start.10
  810.7 2.0 copy-start.5
  812.7 1.2 copy-start.3
  815.7 0.9 copy-start.10
  816.7 2.0 copy-start.5
  818.6 1.2 copy-start.3
  821.7 0.9 copy-start.10
  822.6 2.0 copy-start.5
  824.6 1.2 copy-start.3
  827.6 0.9 copy-start.6
  827.6 0.9 copy-start.10
  828.5 2.0 copy-start.5
  830.5 1.2 copy-start.3
  833.6 0.9 copy-start.10
  834.5 2.0 copy-start.5
  836.5 1.2 copy-start.3
  839.5 0.9 copy-start.6
  839.5 0.9 copy-start.10
  840.4 2.0 copy-start.5
  842.4 1.2 copy-start.3
  845.4 0.9 copy-start.6
  845.4 0.9 copy-start.10
  846.4 2.0 copy-start.5
  848.4 1.2 copy-start.3
  851.4 0.9 copy-start.10
  854.5 317.6 %reduce-scatter.5.cloned.1.call-start = ((), (), s32[]{:S(2)}) async-start(), calls=%async_computation.2 | async-start | bytes 557056 | tf_op jit(solution)/shard_map/reduce_scatter | solution.py:90
  (58 other events, 38.3 us)
Sparse Core Ops, SparseCore 0:
  854.6 251.3 reduce-scatter.6
  1108.8 63.2 reduce-scatter.4
where the time goes:
time: 1180 us
  blocking collectives  617 us (52%)
  waiting for transfers between devices  316 us (27%)
  local copies, waits for them, and re-layouts  133 us (11%)
  other arithmetic  62.3 us (5%)
  matrix products  30.7 us (3%)
  between operations  14.9 us (1%)
    unnamed x3, blocking collectives  337 us
    unnamed x3, waiting for transfers between devices  252 us
    psum x3, blocking collectives, local(): dual_demand = lax.psum(dual_demand, 'adv')  154 us
    all_gather x3, blocking collectives, local(): lax.all_gather(own_prices, 'imp', axis=0, tiled=True)  83 us
    reduce_scatter x1, waiting for transfers between devices, local(): lax.psum_scatter(imp_part, 'adv', scatter_dimension=1, tiled=True)  64.6 us
    all_gather x1, blocking collectives, local(): fetched = lax.all_gather(advertiser_vectors, 'imp', axis=1, tiled=True)  44.2 us
    gather x64, local copies, waits for them, and re-layouts, allocate(): columns = jnp.take(source, chosen, axis=1).reshape(features, extent)  36.6 us
    gather x64, local copies, waits for them, and re-layouts, allocate(): charged = jnp.take(prices, chosen, axis=0).reshape(extent)  35.6 us
  transfers between devices with their start and end apart: 2, of which 2 were waited for; matrix products, arithmetic and copies ran while one was open for 0% of the time, Pallas kernels for 0%

commit v1 on v0

--- a/solution.py
+++ b/solution.py
@@ -2,6 +2,7 @@
 import jax.numpy as jnp
 from jax import lax
 from jax.sharding import PartitionSpec as P
+from jax.lax import all_gather
 
 GROUP = 128
 BLOCK = 128
@@ -61,7 +62,7 @@
         outlay, demand = lax.fori_loop(0, groups_here, advance, totals_start)
         own_outlay = lax.psum_scatter(outlay.reshape(-1), "imp", scatter_dimension=0, tiled=True)
         dual_demand = demand
-        dual_demand = lax.psum(dual_demand, "adv")
+        dual_demand = jnp.sum(all_gather(dual_demand, axis_name="adv"), 0)
         duals = jnp.maximum(duals + dual_demand / capacity - 1.0, 0.0)
         own_prices = jnp.maximum(own_prices + own_outlay / spend_limits - 1.0, 0.0)
         range_prices = lax.all_gather(own_prices, "imp", axis=0, tiled=True).reshape(

time: 1180 us -> 1160 us (0.983)
  the two profiles are of different devices: /device:TPU:25 before, /device:TPU:2 now
where the time goes in v1:
time: 1160 us; the launch traced here: 1150 us
  blocking collectives  630 us (54%)
  waiting for transfers between devices  277 us (24%)
  local copies, waits for them, and re-layouts  134 us (12%)
  other arithmetic  62.4 us (5%)
  matrix products  30.7 us (3%)
  between operations  14.9 us (1%)
    unnamed x3, blocking collectives  404 us
    unnamed x3, waiting for transfers between devices  218 us
    all_gather x3, blocking collectives, local(): lax.all_gather(own_prices, 'imp', axis=0, tiled=True)  121 us
    reduce_scatter x1, waiting for transfers between devices, local(): lax.psum_scatter(imp_part, 'adv', scatter_dimension=1, tiled=True)  59.5 us
    all_gather x1, blocking collectives, local(): fetched = lax.all_gather(advertiser_vectors, 'imp', axis=1, tiled=True)  56.1 us
    all_gather x3, blocking collectives, local(): dual_demand = jnp.sum(all_gather(dual_demand, axis_name='adv'), 0)  48.8 us
    gather x64, local copies, waits for them, and re-layouts, allocate(): columns = jnp.take(source, chosen, axis=1).reshape(features, extent)  36.6 us
    gather x64, local copies, waits for them, and re-layouts, allocate(): charged = jnp.take(prices, chosen, axis=0).reshape(extent)  35.6 us
  transfers between devices with their start and end apart: 2, of which 2 were waited for; matrix products, arithmetic and copies ran while one was open for 0% of the time, Pallas kernels for 0%

profile of v1, /device:TPU:2, one launch (start us, length us, event | category | flops | bytes accessed | tf_op | source)
XLA Modules:
  0.0 1154.9 jit_solution(15267386383275936828)
XLA Ops:
  7.2 0.7 copy-done.12
  8.0 0.7 copy-done.14
  8.8 0.6 copy-done.7
  9.5 56.1 %all_gather.30 = bf16[64,4096]{1,0:T(8,128)(2,1)S(1)} all-gather(bf16[64,128]{1,0:T(8,128)(2,1)S(1)} %copy-done.7), channel_id=1, replica_groups=mesh['imp'=32,'adv'=16] {'imp'}, dimensions={1}, use_global_device_ids=true | all-gather | bytes 540672 | tf_op jit(solution)/shard_map/all_gather | solution.py:24
  65.8 41.5 %while.60 = (s32[]{:T(128)}, f32[32,128]{1,0:T(8,128)S(1)}, f32[2048]{0:T(1024)S(1)}, s32[16,8]{1,0:T(8,128)S(1)}, bf16[64,16,128]{2,0,1:T(8,128)(2,1)S(1)}, /*i...) while((s32[]{:T(128)}, f32[32,128]{1,0:T(8,128)S(1)}, ...), condition=%wide.region_4.7_spmd, body=%wide.region_0.6_spmd.sunk | while | flops 17500104 | bytes 485907 | solution.py:62
  96.3 0.6 scatter_custom_fusion.15
  98.9 0.6 scatter_custom_fusion.15
  107.3 135.6 %all-reduce = f32[4096]{0:T(1024)S(1)} all-reduce(f32[4096]{0:T(1024)S(1)} %bitcast.255), channel_id=5, replica_groups=mesh['imp'=32,'adv'=16] {'imp'}, use_global_device_ids=true, to_apply=%region_5.8.clone | all-reduce | flops 4096 | bytes 32768
  242.9 1.3 dynamic-slice
  244.9 40.1 %all-gather.3 = f32[32,1,128]{2,1,0:T(1,128)S(1)} all-gather(f32[1,1,128]{2,1,0:T(1,128)S(1)} %bitcast.260), channel_id=1, replica_groups=mesh['imp'=32,'adv'=16] {'imp'}, dimensions={0}, use_global_device_ids=true | all-gather | bytes 16896 | tf_op jit(solution)/shard_map/all_gather | solution.py:68
  285.0 17.9 %all-gather = f32[32768]{0:T(1024)S(1)} all-gather(f32[2048]{0:T(1024)S(1)} %get-tuple-element.597), channel_id=2, replica_groups=mesh['imp'=32,'adv'=16] {'adv'}, dimensions={0}, use_global_device_ids=true | all-gather | bytes 139264 | tf_op jit(solution)/shard_map/all_gather | solution.py:65
  303.0 0.7 copy-done.2
  303.7 42.5 %while.61 = (s32[]{:T(128)}, f32[32,128]{1,0:T(8,128)S(1)}, f32[2048]{0:T(1024)S(1)}, s32[16,8]{1,0:T(8,128)S(1)}, bf16[64,16,128]{2,0,1:T(8,128)(2,1)S(1)}, /*i...) while((s32[]{:T(128)}, f32[32,128]{1,0:T(8,128)S(1)}, ...), condition=%wide.region_11.14_spmd, body=%wide.region_7.13_spmd.sunk | while | flops 17631180 | bytes 471067 | solution.py:62
  311.1 0.6 scatter_custom_fusion.17
  324.4 0.6 scatter_custom_fusion.17
  327.1 0.6 scatter_custom_fusion.17
  329.7 0.6 scatter_custom_fusion.17
  346.2 134.6 %all-reduce.1 = f32[4096]{0:T(1024)S(1)} all-reduce(f32[4096]{0:T(1024)S(1)} %bitcast.256), channel_id=6, replica_groups=mesh['imp'=32,'adv'=16] {'imp'}, use_global_device_ids=true, to_apply=%region_12.15.clone | all-reduce | flops 4096 | bytes 32768
  480.8 40.4 %all-gather.4 = f32[32,1,128]{2,1,0:T(1,128)S(1)} all-gather(f32[1,1,128]{2,1,0:T(1,128)S(1)} %bitcast.259), channel_id=1, replica_groups=mesh['imp'=32,'adv'=16] {'imp'}, dimensions={0}, use_global_device_ids=true | all-gather | bytes 16896 | tf_op jit(solution)/shard_map/all_gather | solution.py:68
  521.2 15.3 %all-gather.1 = f32[32768]{0:T(1024)S(1)} all-gather(f32[2048]{0:T(1024)S(1)} %get-tuple-element.599), channel_id=3, replica_groups=mesh['imp'=32,'adv'=16] {'adv'}, dimensions={0}, use_global_device_ids=true | all-gather | bytes 139264 | tf_op jit(solution)/shard_map/all_gather | solution.py:65
  536.6 42.5 %while.62 = (s32[]{:T(128)}, f32[32,128]{1,0:T(8,128)S(1)}, f32[2048]{0:T(1024)S(1)}, s32[16,8]{1,0:T(8,128)S(1)}, bf16[64,16,128]{2,0,1:T(8,128)(2,1)S(1)}, /*i...) while((s32[]{:T(128)}, f32[32,128]{1,0:T(8,128)S(1)}, ...), condition=%wide.region_18.21_spmd, body=%wide.region_14.20_spmd.sunk | while | flops 17631180 | bytes 471067 | solution.py:62
  579.1 134.4 %all-reduce.2 = f32[4096]{0:T(1024)S(1)} all-reduce(f32[4096]{0:T(1024)S(1)} %bitcast.257), channel_id=7, replica_groups=mesh['imp'=32,'adv'=16] {'imp'}, use_global_device_ids=true, to_apply=%region_19.22.clone | all-reduce | flops 4096 | bytes 32768
  714.0 40.2 %all-gather.5 = f32[32,1,128]{2,1,0:T(1,128)S(1)} all-gather(f32[1,1,128]{2,1,0:T(1,128)S(1)} %bitcast.261), channel_id=1, replica_groups=mesh['imp'=32,'adv'=16] {'imp'}, dimensions={0}, use_global_device_ids=true | all-gather | bytes 16896 | tf_op jit(solution)/shard_map/all_gather | solution.py:68
  754.3 15.7 %all-gather.2 = f32[32768]{0:T(1024)S(1)} all-gather(f32[2048]{0:T(1024)S(1)} %get-tuple-element.601), channel_id=4, replica_groups=mesh['imp'=32,'adv'=16] {'adv'}, dimensions={0}, use_global_device_ids=true | all-gather | bytes 139264 | tf_op jit(solution)/shard_map/all_gather | solution.py:65
  770.8 95.1 %while.63 = (s32[]{:T(128)}, f32[64,2048]{1,0:T(8,128)S(1)}, f32[64,32,128]{2,0,1:T(8,128)S(1)}, s32[16,8]{1,0:T(8,128)S(1)}, bf16[64,32,128]{2,0,1:T(8,128)(2,1...) while((s32[]{:T(128)}, f32[64,2048]{1,0:T(8,128)S(1)}, ...), condition=%wide.region_23.26_spmd, body=%wide.region_21.25_spmd.sunk | while | flops 51185740 | bytes 2993603 | solution.py:90
  771.4 0.8 dynamic_slice.201
  775.8 0.9 scatter_fusion
  777.3 0.8 dynamic_slice.201
  781.7 0.9 scatter_fusion
  783.3 0.8 dynamic_slice.201
  787.7 0.9 scatter_fusion
  789.2 0.8 dynamic_slice.201
  793.6 0.9 scatter_fusion
  795.2 0.8 dynamic_slice.201
  799.6 0.9 scatter_fusion
  801.1 0.8 dynamic_slice.201
  805.5 0.9 scatter_fusion
  807.1 0.8 dynamic_slice.201
  811.5 0.9 scatter_fusion
  813.0 0.8 dynamic_slice.201
  817.4 0.9 scatter_fusion
  818.9 0.8 dynamic_slice.201
  823.4 0.9 scatter_fusion
  824.9 0.8 dynamic_slice.201
  829.3 0.9 scatter_fusion
  830.8 0.8 dynamic_slice.201
  835.2 0.9 scatter_fusion
  836.8 0.8 dynamic_slice.201
  841.2 0.9 scatter_fusion
  842.7 0.8 dynamic_slice.201
  847.1 0.9 scatter_fusion
  848.7 0.8 dynamic_slice.201
  853.1 0.9 scatter_fusion
  854.6 0.8 dynamic_slice.201
  859.0 0.9 scatter_fusion
  860.6 0.8 dynamic_slice.201
  865.0 0.9 scatter_fusion
  866.0 0.7 copy-done.1
  866.7 1.3 copy.86
  868.1 0.7 reduce-scatter.5.cloned.1.call-update
  868.8 216.9 %reduce-scatter.7.cloned.1.call-done = bf16[128,64]{1,0:T(8,128)(2,1)} async-done(((bf16[4096,64]{1,0:T(8,128)(2,1)}), bf16[128,64]{1,0:T(8,128)(2,1)}) %reduce-scatter.7.cloned.1.call-update) | async-done | bytes 16400
  1085.7 1.4 copy.85
  1087.2 59.5 %reduce-scatter.5.cloned.1.call-done = f32[64,128]{1,0:T(8,128)} async-done(((f32[64,2048]{1,0:T(8,128)}), f32[64,128]{1,0:T(8,128)}) %reduce-scatter.5.cloned.1.call-update) | async-done | bytes 32784 | tf_op jit(solution)/shard_map/reduce_scatter | solution.py:91
  1146.7 1.4 convert_element_type.23
  (962 shorter events, 188.6 us)
Async XLA Ops:
  7.2 1.6 copy-start
  7.2 1078.5 %reduce-scatter.7.cloned.1.call-start = ((), (), s32[]{:S(2)}) async-start(), calls=%async_computation.3 | async-start | bytes 1081344
  770.8 2.0 copy-start.5
  772.8 1.2 copy-start.3
  775.8 0.9 copy-start.6
  775.8 0.9 copy-start.10
  776.7 2.0 copy-start.5
  778.7 1.2 copy-start.3
  781.7 0.9 copy-start.6
  781.7 0.9 copy-start.10
  782.7 2.0 copy-start.5
  784.6 1.2 copy-start.3
  787.7 0.9 copy-start.6
  787.7 0.9 copy-start.10
  788.6 2.0 copy-start.5
  790.6 1.2 copy-start.3
  793.6 0.9 copy-start.6
  793.6 0.9 copy-start.10
  794.6 2.0 copy-start.5
  796.5 1.2 copy-start.3
  799.6 0.9 copy-start.6
  799.6 0.9 copy-start.10
  800.5 2.0 copy-start.5
  802.5 1.2 copy-start.3
  805.5 0.9 copy-start.6
  805.5 0.9 copy-start.10
  806.5 2.0 copy-start.5
  808.4 1.2 copy-start.3
  811.5 0.9 copy-start.6
  811.5 0.9 copy-start.10
  812.4 2.0 copy-start.5
  814.4 1.2 copy-start.3
  817.4 0.9 copy-start.6
  817.4 0.9 copy-start.10
  818.4 2.0 copy-start.5
  820.3 1.2 copy-start.3
  823.4 0.9 copy-start.6
  823.4 0.9 copy-start.10
  824.3 2.0 copy-start.5
  826.3 1.2 copy-start.3
  829.3 0.9 copy-start.6
  829.3 0.9 copy-start.10
  830.2 2.0 copy-start.5
  832.2 1.2 copy-start.3
  835.2 0.9 copy-start.10
  836.2 2.0 copy-start.5
  838.2 1.2 copy-start.3
  841.2 0.9 copy-start.6
  841.2 0.9 copy-start.10
  842.1 2.0 copy-start.5
  844.1 1.2 copy-start.3
  847.1 0.9 copy-start.6
  847.1 0.9 copy-start.10
  848.1 2.0 copy-start.5
  850.0 1.2 copy-start.3
  853.1 0.9 copy-start.10
  854.0 2.0 copy-start.5
  856.0 1.2 copy-start.3
  859.0 0.9 copy-start.6
  859.0 0.9 copy-start.10
  860.0 2.0 copy-start.5
  861.9 1.2 copy-start.3
  865.0 0.9 copy-start.10
  868.1 278.6 %reduce-scatter.5.cloned.1.call-start = ((), (), s32[]{:S(2)}) async-start(), calls=%async_computation.2 | async-start | bytes 557056 | tf_op jit(solution)/shard_map/reduce_scatter | solution.py:91
  (58 other events, 38.1 us)
Sparse Core Ops, SparseCore 0:
  868.2 217.4 reduce-scatter.6
  1088.5 58.1 reduce-scatter.4
